TPU v7x, 256 devices: a whole 4x4x8 slice. The times are simulated.
256 devices in a mesh: shot: 16 (over x_lo, y, core), rbin: 16 (over x_hi, z).
Axes of the slice: x: 4 (x_hi: 2, x_lo: 2; x = x_hi * 2 + x_lo), y: 4, z: 8, core: 2. Of those that a mesh axis runs over, the one named last changes fastest.
Arguments:
- local_gathers: bfloat16 [2, 2, 8192, 4096], P(None, None, 'shot', 'rbin'), may hold values from -6 to 6
- recorded_shots: bfloat16 [16, 2, 2, 1024, 2048], P('shot', None, None, 'rbin'), may hold values from -0.125 to 0.125
- block_owner: int32 [4], replicated, may hold values from 0 to 15, as said below
- aperture_start: int32 [8192], P('shot'), may hold values from 0 to 4095, as said below
- aperture_end: int32 [8192], P('shot'), may hold values from 1 to 4096
- taper_bin: int32 [4096], P('rbin'), may hold values from 0 to 7
- taper_gain: float32 [8], replicated, may hold values from 0.25 to 1
Outputs:
- multiples: float32 [2, 2048, 2, 8192], P(None, 'rbin', None, 'shot')
Inputs may be any that keep to these rules, and one draw needn't show every extreme that they name: `block_owner`: the 4 entries are distinct. aperture_start < aperture_end for every shot.
All inputs are finite; a program needn't handle non-finite values.
Results may differ from a plain program's by a relative error of at most 0.0029.
Values may be sent and summed in bfloat16 or wider, within the bound.
A program may use at most 128 MiB of HBM per device.

v0:
```python
import jax
import jax.numpy as jnp
from jax import lax
from jax.sharding import PartitionSpec as P

BLOCKS = 4
EDGE = 64


def from_root(value, axis, source):
    kept = jnp.where(lax.axis_index(axis) == source, value, 0).astype(value.dtype)
    return lax.psum(kept, axis)


def taper_weights(columns, aperture_start, aperture_end, taper_bin, taper_gain):
    inside = (columns[None, :] >= aperture_start[:, None]) & (
        columns[None, :] < aperture_end[:, None]
    )
    distance = jnp.minimum(
        columns[None, :] - aperture_start[:, None], aperture_end[:, None] - 1 - columns[None, :]
    )
    ramped = jnp.minimum((distance + 1).astype(jnp.float32) / EDGE, 1.0)
    labels = jnp.arange(taper_gain.shape[0], dtype=jnp.int32)
    bin_gain = jnp.sum(
        jnp.where(taper_bin[:, None] == labels[None, :], taper_gain[None, :], 0.0), axis=1
    )
    return jnp.where(inside, ramped, 0.0) * bin_gain[None, :]


def complex_rows(real_part, imag_part):
    upper_half = jnp.concatenate([real_part, -imag_part], axis=2)
    lower_half = jnp.concatenate([imag_part, real_part], axis=2)
    return jnp.concatenate([upper_half, lower_half], axis=1)


def per_device(
    local_gathers, recorded_shots, block_owner, aperture_start, aperture_end, taper_bin, taper_gain
):
    frequencies, _, shot_count, point_count = local_gathers.shape
    block_width = point_count // BLOCKS
    column_index = lax.axis_index("rbin")
    first_point = column_index * point_count
    columns = first_point + jnp.arange(point_count, dtype=jnp.int32)
    weight = taper_weights(columns, aperture_start, aperture_end, taper_bin, taper_gain)
    tapered = (local_gathers.astype(jnp.float32) * weight[None, None]).astype(jnp.bfloat16)
    own_slot = recorded_shots[0]
    grouped = tapered.reshape(frequencies, 2, shot_count, BLOCKS, block_width)

    def block_rows(block_index):
        return lax.dynamic_index_in_dim(grouped, block_index, 3, keepdims=False)

    out_columns = own_slot.shape[-1]
    accumulated = jnp.zeros((frequencies, out_columns, 2 * shot_count), jnp.float32)
    for position in range(BLOCKS):
        block_index = jnp.int32(position)
        root_device = block_owner[block_index]
        received = from_root(own_slot, "shot", root_device)
        operand = received.reshape(frequencies, -1, out_columns)

        def product(running, operand=operand, block_index=block_index):
            picked = block_rows(block_index)
            left_side = complex_rows(picked[:, 0], picked[:, 1])
            return running + lax.dot_general(
                operand, left_side, (((1,), (2,)), ((0,), (0,))), preferred_element_type=jnp.float32
            )

        accumulated = product(accumulated)
    accumulated = lax.psum_scatter(accumulated, "rbin", scatter_dimension=1, tiled=True)
    return -accumulated.reshape(frequencies, -1, 2, shot_count)


def solution(mesh):
    in_specs = (
        P(None, None, "shot", "rbin"),
        P("shot", None, None, "rbin", None),
        P(),
        P("shot"),
        P("shot"),
        P("rbin"),
        P(),
    )
    out_specs = P(None, "rbin", None, "shot")
    return jax.shard_map(
        per_device, mesh=mesh, in_specs=in_specs, out_specs=out_specs, check_vma=False
    )
```

profile of v0, /device:TPU:1, one launch (start us, length us, event | category | flops | bytes accessed | tf_op | source)
XLA Modules:
  0.0 503.2 jit_solution(17133983559959665374)
XLA Ops:
  6.6 1.5 fusion.40
  10.5 2.5 broadcast_select_fusion
  13.0 2.3 copy.21
  15.3 1.3 copy.24
  16.6 1.3 copy.26
  17.9 1.3 copy.28
  19.3 1.5 copy.22
  20.8 0.1 select_reduce_fusion
  20.9 0.3 select_multiply_fusion
  21.2 0.2 multiply_convert_fusion
  21.4 0.1 fusion.39
  21.5 0.3 copy.30
  21.8 0.3 copy.31
  22.1 0.3 copy.32
  22.4 0.3 copy.33
  22.8 0.8 slice_bitcast_fusion.6
  23.7 133.8 %all-reduce.3.cloned.1.call-done = (bf16[2,128,2048]{1,2,0:T(8,128)(2,1)}, bf16[2,128,2048]{1,2,0:T(8,128)(2,1)}, bf16[2,128,2048]{1,2,0:T(8,128)(2,1)}, bf16[2,128,2048]{1,2,0:T(8,128)(2,1)}) async-done(((bf16[2,128,2048]{1,2,0:T(8,128)(2,1)}, bf16[2,128,2048]{1,2,0:T(8,128)(2,1)}, bf16[2,128,2048]{1,2,0:T(8,128)(2,1)}, bf16[2,128,2048]{1,2,0:T(8,128)(2,1)}), (bf16[2,128,2048]{1,2,0:T(8,128)(2,1)}, ...) | async-done | bytes 4194320 | tf_op jit(solution)/shard_map/psum | solution.py:12
  157.5 9.6 %fusion = f32[2,2048,1024]{2,1,0:T(8,128)} fusion(bf16[2,128,2048]{1,2,0:T(8,128)(2,1)} %get-tuple-element.6, bf16[2,512,64]{2,1,0:T(8,128)(2,1)} %get-tuple-element.22, bf16[2,512,64]{2,1,0:T(8,128)(2,1)S(1)} %get-tuple-element.21, bf16[2,512,64]{2,1,0:T(8,128)(2,1)S(1)} %fusion.35), kind=kOutput, calls=%fused_computation.6 | convolution fusion | flops 1075838976 | bytes 18219008 | tf_op jit(solution)/shard_map/dot_general | solution.py:63
  167.1 8.2 %fusion.8 = f32[2,2048,1024]{2,1,0:T(8,128)} fusion(bf16[2,128,2048]{1,2,0:T(8,128)(2,1)S(1)} %copy-done.2, bf16[2,512,64]{2,1,0:T(8,128)(2,1)S(1)} %get-tuple-element.20, bf16[2,512,64]{2,1,0:T(8,128)(2,1)S(1)} %get-tuple-element.19, bf16[2,512,64]{2,1,0:T(8,128)(2,1)S(1)} %fusion.36), kind=kOutput, calls=%fused_computation.14 | convolution fusion | flops 1075838976 | bytes 18219008 | tf_op jit(solution)/shard_map/dot_general | solution.py:63
  175.3 8.1 %fusion.16 = f32[2,2048,1024]{2,1,0:T(8,128)} fusion(bf16[2,128,2048]{1,2,0:T(8,128)(2,1)S(1)} %copy-done.1, bf16[2,512,64]{2,1,0:T(8,128)(2,1)S(1)} %get-tuple-element.24, bf16[2,512,64]{2,1,0:T(8,128)(2,1)S(1)} %get-tuple-element.23, bf16[2,512,64]{2,1,0:T(8,128)(2,1)S(1)} %fusion.37), kind=kOutput, calls=%fused_computation.22 | convolution fusion | flops 1075838976 | bytes 18219008 | tf_op jit(solution)/shard_map/dot_general | solution.py:63
  183.4 23.0 %add_add_fusion = f32[2,2048,1024]{2,1,0:T(8,128)} fusion(f32[2,2048,1024]{2,1,0:T(8,128)} %fusion.16, f32[2,2048,1024]{2,1,0:T(8,128)} %fusion, f32[2,2048,1024]{2,1,0:T(8,128)} %fusion.8, bf16[2,128,2048]{1,2,0:T(8,128)(2,1)S(1)} %copy-done, bf16[2,512,64]{2,1,0:T(8,128)(2,1)S(1)} %get-tuple-element.18, bf16[2,512,64]{2,1,0:T(8,128)(2,1)S(1)} %get-tuple-element.17, ...), kind=kOutput, calls=%fused_computation | convolution fusion | flops 1088421888 | bytes 68550656 | tf_op jit(solution)/shard_map/dot_general | solution.py:63
  206.5 286.7 %reduce-scatter.2.cloned.1.call-done = f32[2,128,1024]{2,1,0:T(8,128)} async-done(((f32[2,2048,1024]{2,1,0:T(8,128)}), f32[2,128,1024]{2,1,0:T(8,128)}) %reduce-scatter.2.cloned.1.call-update) | async-done | bytes 1048592 | tf_op jit(solution)/shard_map/reduce_scatter | solution.py:68
  493.2 1.3 neg.22
  494.5 1.9 neg.23
  (27 shorter events, 0.4 us)
Async XLA Ops:
  6.5 14.2 %copy-start.5 = (s32[256]{0:T(256)S(1)}, s32[256]{0:T(256)}, u32[]{:S(2)}) copy-start(s32[256]{0:T(256)} %param.12) | copy-start | bytes 3076
  6.5 14.3 %copy-start.6 = (f32[8]{0:T(128)S(1)}, f32[8]{0:T(128)}, u32[]{:S(2)}) copy-start(f32[8]{0:T(128)} %param.13) | copy-start | bytes 100
  6.5 14.3 %copy-start.3 = (s32[512]{0:T(512)S(1)}, s32[512]{0:T(512)}, u32[]{:S(2)}) copy-start(s32[512]{0:T(512)} %param.11) | copy-start | bytes 6148
  6.5 14.4 %copy-start.4 = (s32[512]{0:T(512)S(1)}, s32[512]{0:T(512)}, u32[]{:S(2)}) copy-start(s32[512]{0:T(512)} %param.10) | copy-start | bytes 6148
  6.5 150.9 %all-reduce.3.cloned.1.call-start = ((), (), s32[]{:S(2)}) async-start(), calls=%async_computation.2 | async-start | bytes 8388608 | tf_op jit(solution)/shard_map/psum | solution.py:12
  19.2 474.0 %reduce-scatter.2.cloned.1.call-start = ((), (), s32[]{:S(2)}) async-start(), calls=%async_computation.1 | async-start | bytes 17825792 | tf_op jit(solution)/shard_map/reduce_scatter | solution.py:68
  157.5 9.7 %copy-start.2 = (bf16[2,128,2048]{1,2,0:T(8,128)(2,1)S(1)}, bf16[2,128,2048]{1,2,0:T(8,128)(2,1)}, u32[]{:S(2)}) copy-start(bf16[2,128,2048]{1,2,0:T(8,128)(2,1)} %get-tuple-element.7) | copy-start | bytes 3145732
  157.5 17.8 %copy-start.1 = (bf16[2,128,2048]{1,2,0:T(8,128)(2,1)S(1)}, bf16[2,128,2048]{1,2,0:T(8,128)(2,1)}, u32[]{:S(2)}) copy-start(bf16[2,128,2048]{1,2,0:T(8,128)(2,1)} %get-tuple-element.5) | copy-start | bytes 3145732
  167.1 16.3 %copy-start = (bf16[2,128,2048]{1,2,0:T(8,128)(2,1)S(1)}, bf16[2,128,2048]{1,2,0:T(8,128)(2,1)}, u32[]{:S(2)}) copy-start(bf16[2,128,2048]{1,2,0:T(8,128)(2,1)} %get-tuple-element.8) | copy-start | bytes 3145732
Sparse Core Ops, SparseCore 0:
  19.3 138.0 all-reduce.2
  206.6 286.5 reduce-scatter.1
where the time goes:
time: 503 us
  waiting for transfers between devices  420 us (83%)
  matrix products  49 us (10%)
  between operations  16 us (3%)
  local copies, waits for them, and re-layouts  13.1 us (3%)
    reduce_scatter x1, waiting for transfers between devices, per_device(): lax.psum_scatter(accumulated, 'rbin', scatter_dimension=1, tiled=True)  287 us
    psum x1, waiting for transfers between devices, from_root(): return lax.psum(kept, axis)  134 us
    dot_general x4, matrix products, product(): lax.dot_general(operand, left_side, (((1,), (2,)), ((0,), (0,))), preferr...  49 us
  transfers between devices with their start and end apart: 2, of which 2 were waited for; matrix products, arithmetic and copies ran while one was open for 1% of the time, Pallas kernels for 0%

commit v1 on v0

--- a/solution.py
+++ b/solution.py
@@ -9,7 +9,7 @@
 
 def from_root(value, axis, source):
     kept = jnp.where(lax.axis_index(axis) == source, value, 0).astype(value.dtype)
-    return lax.psum(kept, axis)
+    return jnp.sum(lax.all_gather(kept, axis), axis=0)
 
 
 def taper_weights(columns, aperture_start, aperture_end, taper_bin, taper_gain):

time: 503 us -> 732 us (1.46)
  waiting for transfers between devices: 420 us -> 609 us
  other arithmetic: 4.54 us -> 46.9 us
    all_gather x0 -> x4, waiting for transfers between devices: none -> 321 us  [from_root(): return jnp.sum(lax.all_gather(kept, axis), axis=0)]
    psum x1 -> x0, waiting for transfers between devices: 134 us -> none  [from_root(): return lax.psum(kept, axis)]
    reduce_sum x0 -> x4, other arithmetic: none -> 37.4 us  [from_root(): return jnp.sum(lax.all_gather(kept, axis), axis=0)]
  transfers between devices with their start and end apart: 2 -> 5, of which waited for: 2 -> 5; matrix products, arithmetic and copies ran while one was open for 1% -> 9% of each run, Pallas kernels for 0% -> 0%
where the time goes in v1:
time: 732 us
  waiting for transfers between devices  609 us (83%)
  matrix products  50.7 us (7%)
  other arithmetic  46.9 us (6%)
  between operations  15.8 us (2%)
  local copies, waits for them, and re-layouts  9.35 us (1%)
    all_gather x4, waiting for transfers between devices, from_root(): return jnp.sum(lax.all_gather(kept, axis), axis=0)  321 us
    reduce_scatter x1, waiting for transfers between devices, per_device(): lax.psum_scatter(accumulated, 'rbin', scatter_dimension=1, tiled=True)  286 us
    dot_general x4, matrix products, product(): lax.dot_general(operand, left_side, (((1,), (2,)), ((0,), (0,))), preferr...  50.7 us
    reduce_sum x4, other arithmetic, from_root(): return jnp.sum(lax.all_gather(kept, axis), axis=0)  37.4 us
  transfers between devices with their start and end apart: 5, of which 5 were waited for; matrix products, arithmetic and copies ran while one was open for 9% of the time, Pallas kernels for 0%

profile of v1, /device:TPU:1, one launch (start us, length us, event | category | flops | bytes accessed | tf_op | source)
XLA Modules:
  0.0 731.7 jit_solution(3014049557155877532)
XLA Ops:
  6.5 1.4 fusion.40
  10.4 3.3 broadcast_select_fusion
  15.9 1.5 copy.26
  17.4 0.8 select_reduce_fusion
  18.9 1.0 select_multiply_fusion
  23.6 0.8 slice_bitcast_fusion
  24.4 0.9 slice_bitcast_fusion.2
  25.2 0.8 slice_bitcast_fusion.4
  26.1 0.8 slice_bitcast_fusion.6
  26.9 85.4 %all-gather.7.cloned.1.call-done = bf16[16,2,2,64,2048]{4,3,2,1,0:T(8,128)(2,1)} async-done(((bf16[1,2,2,64,2048]{4,3,2,1,0:T(8,128)(2,1)}), bf16[16,2,2,64,2048]{4,3,2,1,0:T(8,128)(2,1)}) %all-gather.7.cloned.1.call-update) | async-done | bytes 16777232 | tf_op jit(solution)/shard_map/all_gather | solution.py:12
  112.3 9.3 %reduce_sum.59 = bf16[2,2,64,2048]{3,2,1,0:T(8,128)(2,1)S(1)} reduce(bf16[16,2,2,64,2048]{4,3,2,1,0:T(8,128)(2,1)} %all-gather.7.cloned.1.call-done, bf16[]{:T(256)} %constant.38.clone.1), dimensions={0}, to_apply=%region_2.3 | reduce | flops 7864320 | bytes 17825794 | tf_op jit(solution)/shard_map/reduce_sum | solution.py:12
  121.6 87.7 %all-gather.5.cloned.1.call-done = bf16[16,2,2,64,2048]{4,3,2,1,0:T(8,128)(2,1)} async-done(((bf16[1,2,2,64,2048]{4,3,2,1,0:T(8,128)(2,1)}), bf16[16,2,2,64,2048]{4,3,2,1,0:T(8,128)(2,1)}) %all-gather.5.cloned.1.call-update) | async-done | bytes 16777232 | tf_op jit(solution)/shard_map/all_gather | solution.py:12
  209.3 9.3 %reduce_sum.57 = bf16[2,2,64,2048]{3,2,1,0:T(8,128)(2,1)S(1)} reduce(bf16[16,2,2,64,2048]{4,3,2,1,0:T(8,128)(2,1)} %all-gather.5.cloned.1.call-done, bf16[]{:T(256)} %constant.38.clone.1), dimensions={0}, to_apply=%region_0.1 | reduce | flops 7864320 | bytes 17825794 | tf_op jit(solution)/shard_map/reduce_sum | solution.py:12
  218.6 87.7 %all-gather.9.cloned.1.call-done = bf16[16,2,2,64,2048]{4,3,2,1,0:T(8,128)(2,1)} async-done(((bf16[1,2,2,64,2048]{4,3,2,1,0:T(8,128)(2,1)}), bf16[16,2,2,64,2048]{4,3,2,1,0:T(8,128)(2,1)}) %all-gather.9.cloned.1.call-update) | async-done | bytes 16777232 | tf_op jit(solution)/shard_map/all_gather | solution.py:12
  306.4 9.3 %reduce_sum.60 = bf16[2,2,64,2048]{3,2,1,0:T(8,128)(2,1)S(1)} reduce(bf16[16,2,2,64,2048]{4,3,2,1,0:T(8,128)(2,1)} %all-gather.9.cloned.1.call-done, bf16[]{:T(256)} %constant.38.clone.1), dimensions={0}, to_apply=%region_3.4 | reduce | flops 7864320 | bytes 17825794 | tf_op jit(solution)/shard_map/reduce_sum | solution.py:12
  315.7 10.1 %fusion.16 = f32[2,2048,1024]{2,1,0:T(8,128)} fusion(bf16[2,128,2048]{2,1,0:T(8,128)(2,1)S(1)} %bitcast.44, bf16[2,512,64]{2,1,0:T(8,128)(2,1)} %get-tuple-element.20, bf16[2,512,64]{2,1,0:T(8,128)(2,1)} %get-tuple-element.19, bf16[2,512,64]{2,1,0:T(8,128)(2,1)} %fusion.37), kind=kOutput, calls=%fused_computation.22 | convolution fusion | flops 1075838976 | bytes 18219008 | tf_op jit(solution)/shard_map/dot_general | solution.py:63
  325.9 8.5 %fusion = f32[2,2048,1024]{2,1,0:T(8,128)} fusion(bf16[2,128,2048]{2,1,0:T(8,128)(2,1)S(1)} %bitcast.43, bf16[2,512,64]{2,1,0:T(8,128)(2,1)S(1)} %copy-done.7, bf16[2,512,64]{2,1,0:T(8,128)(2,1)S(1)} %copy-done.6, bf16[2,512,64]{2,1,0:T(8,128)(2,1)S(1)} %copy-done.1), kind=kOutput, calls=%fused_computation.6 | convolution fusion | flops 1075838976 | bytes 18219008 | tf_op jit(solution)/shard_map/dot_general | solution.py:63
  334.4 8.4 %fusion.8 = f32[2,2048,1024]{2,1,0:T(8,128)} fusion(bf16[2,128,2048]{2,1,0:T(8,128)(2,1)S(1)} %bitcast.42, bf16[2,512,64]{2,1,0:T(8,128)(2,1)S(1)} %copy-done.5, bf16[2,512,64]{2,1,0:T(8,128)(2,1)S(1)} %copy-done.4, bf16[2,512,64]{2,1,0:T(8,128)(2,1)S(1)} %copy-done), kind=kOutput, calls=%fused_computation.14 | convolution fusion | flops 1075838976 | bytes 18219008 | tf_op jit(solution)/shard_map/dot_general | solution.py:63
  342.9 60.4 %all-gather.11.cloned.1.call-done = bf16[16,2,2,64,2048]{4,3,2,1,0:T(8,128)(2,1)} async-done(((bf16[1,2,2,64,2048]{4,3,2,1,0:T(8,128)(2,1)}), bf16[16,2,2,64,2048]{4,3,2,1,0:T(8,128)(2,1)}) %all-gather.11.cloned.1.call-update) | async-done | bytes 16777232 | tf_op jit(solution)/shard_map/all_gather | solution.py:12
  403.3 9.5 %reduce_sum.61 = bf16[2,2,64,2048]{3,2,1,0:T(8,128)(2,1)S(1)} reduce(bf16[16,2,2,64,2048]{4,3,2,1,0:T(8,128)(2,1)} %all-gather.11.cloned.1.call-done, bf16[]{:T(256)} %constant.38.clone.1), dimensions={0}, to_apply=%region_4.5 | reduce | flops 7864320 | bytes 17825794 | tf_op jit(solution)/shard_map/reduce_sum | solution.py:12
  412.8 23.6 %add_add_fusion = f32[2,2048,1024]{2,1,0:T(8,128)} fusion(f32[2,2048,1024]{2,1,0:T(8,128)} %fusion.16, f32[2,2048,1024]{2,1,0:T(8,128)} %fusion, f32[2,2048,1024]{2,1,0:T(8,128)} %fusion.8, bf16[2,128,2048]{2,1,0:T(8,128)(2,1)S(1)} %bitcast.41, bf16[2,512,64]{2,1,0:T(8,128)(2,1)S(1)} %copy-done.3, bf16[2,512,64]{2,1,0:T(8,128)(2,1)S(1)} %copy-done.2, ...), kind=kOutput, calls=%fused_computation | convolution fusion | flops 1088421888 | bytes 68550656 | tf_op jit(solution)/shard_map/dot_general | solution.py:63
  436.4 285.6 %reduce-scatter.2.cloned.1.call-done = f32[2,128,1024]{2,1,0:T(8,128)} async-done(((f32[2,2048,1024]{2,1,0:T(8,128)}), f32[2,128,1024]{2,1,0:T(8,128)}) %reduce-scatter.2.cloned.1.call-update) | async-done | bytes 1048592 | tf_op jit(solution)/shard_map/reduce_scatter | solution.py:68
  722.0 1.3 neg.22
  723.3 1.9 neg.23
  (38 shorter events, 6.5 us)
Async XLA Ops:
  6.5 105.8 %all-gather.7.cloned.1.call-start = ((), (), s32[]{:S(2)}) async-start(), calls=%async_computation.2 | async-start | bytes 17825792 | tf_op jit(solution)/shard_map/all_gather | solution.py:12
  13.8 195.6 %all-gather.5.cloned.1.call-start = ((), (), s32[]{:S(2)}) async-start(), calls=%async_computation.1 | async-start | bytes 17825792 | tf_op jit(solution)/shard_map/all_gather | solution.py:12
  14.5 291.9 %all-gather.9.cloned.1.call-start = ((), (), s32[]{:S(2)}) async-start(), calls=%async_computation.3 | async-start | bytes 17825792 | tf_op jit(solution)/shard_map/all_gather | solution.py:12
  15.3 388.0 %all-gather.11.cloned.1.call-start = ((), (), s32[]{:S(2)}) async-start(), calls=%async_computation.4 | async-start | bytes 17825792 | tf_op jit(solution)/shard_map/all_gather | solution.py:12
  15.8 706.2 %reduce-scatter.2.cloned.1.call-start = ((), (), s32[]{:S(2)}) async-start(), calls=%async_computation.5 | async-start | bytes 17825792 | tf_op jit(solution)/shard_map/reduce_scatter | solution.py:68
  315.7 10.2 %copy-start.1 = (bf16[2,512,64]{2,1,0:T(8,128)(2,1)S(1)}, bf16[2,512,64]{2,1,0:T(8,128)(2,1)}, u32[]{:S(2)}) copy-start(bf16[2,512,64]{2,1,0:T(8,128)(2,1)} %fusion.35) | copy-start | bytes 393220
  315.7 10.2 %copy-start.6 = (bf16[2,512,64]{2,1,0:T(8,128)(2,1)S(1)}, bf16[2,512,64]{2,1,0:T(8,128)(2,1)}, u32[]{:S(2)}) copy-start(bf16[2,512,64]{2,1,0:T(8,128)(2,1)} %get-tuple-element.17) | copy-start | bytes 393220
  315.7 10.2 %copy-start.7 = (bf16[2,512,64]{2,1,0:T(8,128)(2,1)S(1)}, bf16[2,512,64]{2,1,0:T(8,128)(2,1)}, u32[]{:S(2)}) copy-start(bf16[2,512,64]{2,1,0:T(8,128)(2,1)} %get-tuple-element.18) | copy-start | bytes 393220
  315.7 18.7 %copy-start = (bf16[2,512,64]{2,1,0:T(8,128)(2,1)S(1)}, bf16[2,512,64]{2,1,0:T(8,128)(2,1)}, u32[]{:S(2)}) copy-start(bf16[2,512,64]{2,1,0:T(8,128)(2,1)} %fusion.36) | copy-start | bytes 393220
  315.7 18.7 %copy-start.4 = (bf16[2,512,64]{2,1,0:T(8,128)(2,1)S(1)}, bf16[2,512,64]{2,1,0:T(8,128)(2,1)}, u32[]{:S(2)}) copy-start(bf16[2,512,64]{2,1,0:T(8,128)(2,1)} %get-tuple-element.15) | copy-start | bytes 393220
  315.7 18.7 %copy-start.5 = (bf16[2,512,64]{2,1,0:T(8,128)(2,1)S(1)}, bf16[2,512,64]{2,1,0:T(8,128)(2,1)}, u32[]{:S(2)}) copy-start(bf16[2,512,64]{2,1,0:T(8,128)(2,1)} %get-tuple-element.16) | copy-start | bytes 393220
  334.4 78.3 %copy-start.2 = (bf16[2,512,64]{2,1,0:T(8,128)(2,1)S(1)}, bf16[2,512,64]{2,1,0:T(8,128)(2,1)}, u32[]{:S(2)}) copy-start(bf16[2,512,64]{2,1,0:T(8,128)(2,1)} %get-tuple-element.13) | copy-start | bytes 393220
  334.4 78.4 %copy-start.3 = (bf16[2,512,64]{2,1,0:T(8,128)(2,1)S(1)}, bf16[2,512,64]{2,1,0:T(8,128)(2,1)}, u32[]{:S(2)}) copy-start(bf16[2,512,64]{2,1,0:T(8,128)(2,1)} %get-tuple-element.14) | copy-start | bytes 393220
Sparse Core Ops, SparseCore 0:
  13.9 98.3 all-gather.6
  114.2 95.1 all-gather.4
  211.2 95.1 all-gather.8
  308.1 95.1 all-gather.10
  436.5 285.4 reduce-scatter.1
